TPU v7x, 32 devices: a whole 2x2x4 slice. The times are simulated.
32 devices in a mesh: dp: 16 (over z, x, core), axial: 2 (over y).
Axes of the slice: x: 2, y: 2, z: 4, core: 2. Of those that a mesh axis runs over, the one named last changes fastest.
Arguments:
- homolog_activations: bfloat16 [16, 32, 16, 256], P('dp', None, 'axial'), may hold values from -6 to 6
- homolog_adjoint: bfloat16 [16, 32, 16, 256], P('dp', None, 'axial'), may hold values from -6 to 6
- duplex_adjoint: bfloat16 [16, 16, 16, 128], P('dp', 'axial'), may hold values from -6 to 6
- homolog_exists_filter: int32 [16, 32], P('dp'), may hold values 0 or 1
- amino_exists_filter: int32 [16, 16], P('dp'), may hold values 0 or 1
- focus_matrices_tier: bfloat16 [5, 256, 256], replicated, may hold values from -0.375 to 0.375
- affine_parameters: float32 [5, 256], replicated, may hold values from -1.5 to 1.75, as said below
- left_right_matrices: bfloat16 [256, 64], replicated, may hold values from -0.375 to 0.375
- outer_final_matrix: bfloat16 [1024, 128], replicated, may hold values from -0.1875 to 0.1875
Outputs:
- homolog_derivative: bfloat16 [16, 32, 16, 256], P('dp', None, 'axial')
- grad_attention: float32 [5, 256, 256], replicated
- grad_vectors: float32 [5, 256], replicated
- grad_proj: float32 [256, 64], replicated
- pair_weight_gradient: float32 [1024, 128], replicated
Inputs may be any that keep to these rules, and one draw needn't show every extreme that they name: `affine_parameters`: gains near one, biases near zero.
All inputs are finite; a program needn't handle non-finite values. No bound on the sum of `homolog_exists_filter` or of `amino_exists_filter` on one device may be relied on, other than what follows from the above.
Results may differ from a plain program's by a relative error of at most 0.018.
Values may be sent and summed in bfloat16 or wider, within the bound.
No kernel may reach another device: no remote copies, remote signals or barrier semaphores. Data moves between devices by JAX's collectives and lax.ppermute only.
A program may use at most 64 MiB of HBM per device.

v0:
```python
from functools import partial
import jax
import jax.numpy as jnp
from jax import lax
from jax.sharding import PartitionSpec as P

HEADS = 8
HEAD_DIM = 32
OUTER_FACTORS = 32
DUPLEX_FEATURES = 128


def layer_normalize(values, scale_row, shift_row):
    average = jnp.mean(values, axis=-1, keepdims=True)
    centered = values - average
    spread = jnp.mean(centered * centered, axis=-1, keepdims=True)
    return centered * lax.rsqrt(spread + 1e-05) * scale_row + shift_row


def column_attention_block(
    sequence_flags,
    residue_flags,
    alignment_block,
    focus_matrices_tier,
    affine_parameters,
    left_right_matrices,
):
    sequence_total, present_row_count, channel_width = alignment_block.shape
    normalized_input = layer_normalize(
        alignment_block.astype(jnp.float32), affine_parameters[0], affine_parameters[1]
    ).astype(jnp.bfloat16)
    flat_rows = normalized_input.reshape(sequence_total * present_row_count, channel_width)
    shape_heads = (sequence_total, present_row_count, HEADS, HEAD_DIM)
    queries = (
        (
            jnp.dot(flat_rows, focus_matrices_tier[0], preferred_element_type=jnp.float32)
            * HEAD_DIM ** (-0.5)
        )
        .astype(jnp.bfloat16)
        .reshape(shape_heads)
    )
    keys_all = (
        jnp.dot(flat_rows, focus_matrices_tier[1], preferred_element_type=jnp.float32)
        .astype(jnp.bfloat16)
        .reshape(shape_heads)
    )
    values_all = (
        jnp.dot(flat_rows, focus_matrices_tier[2], preferred_element_type=jnp.float32)
        .astype(jnp.bfloat16)
        .reshape(shape_heads)
    )
    gate_value = jax.nn.sigmoid(
        jnp.dot(flat_rows, focus_matrices_tier[3], preferred_element_type=jnp.float32)
        + affine_parameters[2]
    )
    logits = jnp.einsum("srhd,trhd->rhst", queries, keys_all, preferred_element_type=jnp.float32)
    mask_bias = (sequence_flags.astype(jnp.float32) - 1.0) * 1000000000.0
    probs = jax.nn.softmax(logits + mask_bias[None, None, None, :], axis=-1).astype(jnp.bfloat16)
    attended = jnp.einsum("rhst,trhd->srhd", probs, values_all, preferred_element_type=jnp.float32)
    gated = (
        attended.reshape(sequence_total * present_row_count, channel_width) * gate_value
    ).astype(jnp.bfloat16)
    rows_update = jnp.dot(gated, focus_matrices_tier[4], preferred_element_type=jnp.float32)
    updated_alignment = alignment_block.astype(jnp.float32) + rows_update.reshape(
        sequence_total, present_row_count, channel_width
    )
    second = (
        layer_normalize(updated_alignment, affine_parameters[3], affine_parameters[4])
        .astype(jnp.bfloat16)
        .reshape(sequence_total * present_row_count, channel_width)
    )
    projected = jnp.dot(second, left_right_matrices, preferred_element_type=jnp.float32).reshape(
        sequence_total, present_row_count, 2 * OUTER_FACTORS
    )
    flags = (sequence_flags[:, None] * residue_flags[None, :]).astype(jnp.float32)
    projected = (projected * flags[:, :, None]).astype(jnp.bfloat16)
    return (updated_alignment, projected[:, :, :OUTER_FACTORS], projected[:, :, OUTER_FACTORS:])


def pair_block(left_part, right_part, outer_final_matrix, flags_rows, flags_cols, seq_total):
    outer = jnp.einsum("sic,sje->ijce", left_part, right_part, precision=lax.Precision.HIGHEST)
    rows_i, cols_j = (outer.shape[0], outer.shape[1])
    outer_flat = outer.reshape(rows_i * cols_j, OUTER_FACTORS * OUTER_FACTORS).astype(jnp.bfloat16)
    pair_rows = jnp.dot(outer_flat, outer_final_matrix, preferred_element_type=jnp.float32).reshape(
        rows_i, cols_j, DUPLEX_FEATURES
    )
    divisor = jnp.maximum(flags_rows[:, None] * flags_cols[None, :] * seq_total, 1.0)
    return pair_rows / divisor[:, :, None]


def per_device(
    homolog_activations,
    homolog_adjoint,
    duplex_adjoint,
    homolog_exists_filter,
    amino_exists_filter,
    focus_matrices_tier,
    affine_parameters,
    left_right_matrices,
    outer_final_matrix,
):
    shard_homologs = homolog_activations[0]
    local_cotangent = homolog_adjoint[0]
    pair_update_cotangent = duplex_adjoint[0]
    sequence_flags = homolog_exists_filter[0]
    residue_flags = amino_exists_filter[0]
    present_row_count = shard_homologs.shape[1]
    own_index = lax.axis_index("axial")
    own_flags = lax.dynamic_slice_in_dim(
        residue_flags, own_index * present_row_count, present_row_count
    )
    seq_total = jnp.sum(sequence_flags.astype(jnp.float32))
    res_float = residue_flags.astype(jnp.float32)
    own_float = own_flags.astype(jnp.float32)
    local_function = partial(column_attention_block, sequence_flags, own_flags)
    step_outputs, backward_function = jax.vjp(
        local_function, shard_homologs, focus_matrices_tier, affine_parameters, left_right_matrices
    )
    left_own, right_own = lax.optimization_barrier((step_outputs[1], step_outputs[2]))
    left_float = left_own.astype(jnp.float32)
    right_all = lax.all_gather(right_own, "axial", axis=1, tiled=True)

    def pair_fn(left_part, right_part, weight_part):
        return pair_block(left_part, right_part, weight_part, own_float, res_float, seq_total)

    unused, back_pair = jax.vjp(
        pair_fn, left_float, right_all.astype(jnp.float32), outer_final_matrix
    )
    left_cot, right_cot, pair_weight_cot = back_pair(pair_update_cotangent.astype(jnp.float32))
    right_grad = lax.psum_scatter(
        right_cot.astype(jnp.bfloat16), "axial", scatter_dimension=1, tiled=True
    )
    pair_weight_gradient = pair_weight_cot.astype(jnp.float32)
    cotangent_list = (
        local_cotangent.astype(jnp.float32),
        left_cot.astype(jnp.bfloat16),
        right_grad,
    )
    alignment_piece, attention_piece, vector_piece, projection_piece = backward_function(
        cotangent_list
    )
    focus_derivative = attention_piece.astype(jnp.float32)
    affine_derivative = vector_piece
    factor_derivative = projection_piece.astype(jnp.float32)
    focus_derivative, affine_derivative, factor_derivative, pair_weight_gradient = lax.psum(
        (focus_derivative, affine_derivative, factor_derivative, pair_weight_gradient),
        ("dp", "axial"),
    )
    return (
        alignment_piece[None],
        focus_derivative,
        affine_derivative,
        factor_derivative,
        pair_weight_gradient,
    )


def solution(mesh):
    return jax.shard_map(
        per_device,
        mesh=mesh,
        in_specs=(
            P("dp", None, "axial", None),
            P("dp", None, "axial", None),
            P("dp", "axial", None, None),
            P("dp", None),
            P("dp", None),
            P(),
            P(),
            P(),
            P(),
        ),
        out_specs=(P("dp", None, "axial", None), P(), P(), P(), P()),
        check_vma=False,
    )
```

profile of v0, /device:TPU:0, one launch (start us, length us, event | category | flops | bytes accessed | tf_op | source)
XLA Modules:
  0.0 220.5 jit_solution(12519017308732594654)
XLA Ops:
  7.2 1.1 convert_reduce_fusion
  8.3 1.1 fusion.48
  9.4 1.5 fusion.131
  10.9 1.2 fusion.11
  12.1 1.2 convolution_convert_fusion.18
  13.4 1.2 convolution_convert_fusion.19
  15.1 0.7 add_multiply_fusion
  16.1 0.8 fusion.133
  18.7 0.9 copy.86
  20.4 1.9 multiply_convert_fusion
  22.3 1.2 fusion.134
  24.9 0.7 fusion.130
  25.9 0.7 multiply_maximum_fusion.1
  26.9 0.8 reshape.446
  28.0 0.8 reshape.467
  28.9 0.6 copy.88
  29.5 1.4 multiply_divide_fusion
  30.9 2.0 multiply_maximum_fusion
  32.9 6.3 %all_gather.3 = bf16[32,16,32]{2,1,0:T(8,128)(2,1)S(1)} all-gather(bf16[32,8,32]{2,1,0:T(8,128)(2,1)} %get-tuple-element.8), channel_id=1, replica_groups=mesh['dp'=16,'axial'=2] {'axial'}, dimensions={1}, use_global_device_ids=true | all-gather | bytes 49152 | tf_op jit(solution)/shard_map/all_gather | solution.py:121
  39.3 0.7 copy-done.10
  39.9 2.3 %fusion = bf16[8,16,32,32]{2,3,0,1:T(8,128)(2,1)} fusion(bf16[32,16,32,1]{2,1,0,3:T(8,128)(2,1)S(1)} %bitcast.263, bf16[32,8,32]{2,1,0:T(8,128)(2,1)} %copy-done.18), kind=kOutput, calls=%fused_computation.1 | convolution fusion | flops 8519680 | bytes 311296 | tf_op jit(solution)/shard_map/jvp(sic,sje->ijce)/dot_general | solution.py:81
  42.2 1.6 copy.105
  43.8 1.8 convert_element_type.291
  45.6 0.9 broadcast_divide_fusion
  46.5 2.0 fusion.6
  48.5 1.4 convolution_bitcast_fusion.2
  50.0 0.6 div.102
  50.7 0.8 reshape.468
  51.7 0.8 fusion.69
  52.9 1.8 fusion.135
  55.0 0.6 copy.94
  55.6 1.2 fusion.4
  56.8 0.6 fusion.31
  57.9 1.5 fusion.5
  59.4 1.5 fusion.3
  60.9 1.2 fusion.126
  62.1 1.9 copy.96
  64.4 0.9 convolution_convert_fusion.16
  65.3 1.2 copy.99
  66.9 0.9 convolution_convert_fusion.15
  68.7 1.4 fusion.51
  70.3 1.0 fusion.27
  73.1 1.2 add_convert_fusion
  75.0 41.5 %psum.29 = f32[5,256]{1,0:T(8,128)} all-reduce(f32[5,256]{1,0:T(8,128)S(1)} %pad_add_fusion.3), channel_id=1, replica_groups=mesh['dp'=16,'axial'=2] {'dp','axial'}, use_global_device_ids=true, to_apply=%region_19.0 | all-reduce | flops 1280 | bytes 10240 | tf_op jit(solution)/shard_map/psum | solution.py:145
  116.4 0.9 fusion.73
  117.3 92.3 %all-reduce.15.cloned.1.call-done = (f32[5,256,256]{2,1,0:T(8,128)}, f32[256,64]{0,1:T(8,128)}, f32[1024,128]{1,0:T(8,128)}) async-done(((f32[5,256,256]{2,1,0:T(8,128)}, f32[256,64]{0,1:T(8,128)}, f32[1024,128]{1,0:T(8,128)}), (f32[5,256,256]{2,1,0:T(8,128)}, f32[256,64]{0,1:T(8,128)}, f32[1024,128]{1,0:T(8,128)})) %all-reduce.15.cloned.1.call-update) | async-done | bytes 1900560 | tf_op jit(solution)/shard_map/psum | solution.py:145
  209.7 2.6 %copy.154 = f32[5,256,256]{2,1,0:T(8,128)} copy(f32[5,256,256]{2,1,0:T(8,128)} %get-tuple-element.52) | data formatting | bytes 2621440
  212.9 0.8 copy.156
  (208 shorter events, 11.3 us)
Async XLA Ops:
  7.2 19.5 %copy-start = (bf16[1024,128]{1,0:T(8,128)(2,1)S(1)}, bf16[1024,128]{1,0:T(8,128)(2,1)}, u32[]{:S(2)}) copy-start(bf16[1024,128]{1,0:T(8,128)(2,1)} %param.17) | copy-start | bytes 786436
  7.2 6.2 %copy-start.1 = (bf16[1,32,8,256]{3,2,1,0:T(8,128)(2,1)S(1)}, bf16[1,32,8,256]{3,2,1,0:T(8,128)(2,1)}, u32[]{:S(2)}) copy-start(bf16[1,32,8,256]{3,2,1,0:T(8,128)(2,1)} %param.9) | copy-start | bytes 393220
  7.2 43.5 %reduce-scatter.4.cloned.1.call-start = ((), (), s32[]{:S(2)}) async-start(), calls=%async_computation.1 | async-start | bytes 49152
  9.4 5.2 %copy-start.27 = (f32[32,8]{1,0:T(8,128)}, f32[32,8]{1,0:T(8,128)S(1)}, u32[]{:S(2)}) copy-start(f32[32,8]{1,0:T(8,128)S(1)} %fusion.48) | copy-start | bytes 3076
  9.4 5.4 %copy-start.38 = (f32[32,8]{1,0:T(8,128)}, f32[32,8]{1,0:T(8,128)S(1)}, u32[]{:S(2)}) copy-start(f32[32,8]{1,0:T(8,128)S(1)} %fusion.115) | copy-start | bytes 3076
  10.9 3.9 %copy-start.53 = (f32[1,256]{1,0:T(1,128)}, f32[1,256]{1,0:T(1,128)S(1)}, u32[]{:S(2)}) copy-start(f32[1,256]{1,0:T(1,128)S(1)} %get-tuple-element.31) | copy-start | bytes 3076
  10.9 3.9 %copy-start.65 = (f32[1,256]{1,0:T(1,128)}, f32[1,256]{1,0:T(1,128)S(1)}, u32[]{:S(2)}) copy-start(f32[1,256]{1,0:T(1,128)S(1)} %get-tuple-element.30) | copy-start | bytes 3076
  12.1 3.0 %copy-start.72 = (s32[1,32]{1,0:T(1,128)S(1)}, s32[1,32]{1,0:T(1,128)}, u32[]{:S(2)}) copy-start(s32[1,32]{1,0:T(1,128)} %param.12) | copy-start | bytes 388
  20.0 3.8 %copy-start.12 = (f32[256,256]{1,0:T(8,128)}, f32[256,256]{1,0:T(8,128)S(1)}, u32[]{:S(2)}) copy-start(f32[256,256]{1,0:T(8,128)S(1)} %reshape.445) | copy-start | bytes 786436
  20.3 3.4 %copy-start.74 = (s32[1,16]{1,0:T(1,128)S(1)}, s32[1,16]{1,0:T(1,128)}, u32[]{:S(2)}) copy-start(s32[1,16]{1,0:T(1,128)} %param.13) | copy-start | bytes 196
  20.3 3.5 %copy-start.73 = (s32[1,32]{1,0:T(1,128)S(1)}, s32[1,32]{1,0:T(1,128)}, u32[]{:S(2)}) copy-start(s32[1,32]{1,0:T(1,128)} %param.12) | copy-start | bytes 388
  20.3 4.3 %copy-start.58 = (f32[1,256]{1,0:T(1,128)S(1)}, f32[1,256]{1,0:T(1,128)}, u32[]{:S(2)}) copy-start(f32[1,256]{1,0:T(1,128)} %get-tuple-element.28) | copy-start | bytes 3076
  20.4 4.3 %copy-start.68 = (f32[1,256]{1,0:T(1,128)S(1)}, f32[1,256]{1,0:T(1,128)}, u32[]{:S(2)}) copy-start(f32[1,256]{1,0:T(1,128)} %get-tuple-element.32) | copy-start | bytes 3076
  20.4 4.3 %copy-start.75 = (bf16[256,64]{0,1:T(8,128)(2,1)S(1)}, bf16[256,64]{0,1:T(8,128)(2,1)}, u32[]{:S(2)}) copy-start(bf16[256,64]{0,1:T(8,128)(2,1)} %param.16) | copy-start | bytes 98308
  22.3 4.4 %copy-start.21 = (bf16[256,256]{1,0:T(8,128)(2,1)}, bf16[256,256]{1,0:T(8,128)(2,1)S(1)}, u32[]{:S(2)}) copy-start(bf16[256,256]{1,0:T(8,128)(2,1)S(1)} %get-tuple-element.39) | copy-start | bytes 393220
  22.3 4.3 %copy-start.36 = (bf16[1,8,16,128]{3,2,1,0:T(8,128)(2,1)S(1)}, bf16[1,8,16,128]{3,2,1,0:T(8,128)(2,1)}, u32[]{:S(2)}) copy-start(bf16[1,8,16,128]{3,2,1,0:T(8,128)(2,1)} %param.11) | copy-start | bytes 98308
  23.5 3.2 %copy-start.2 = (f32[32,8,256]{2,1,0:T(8,128)}, f32[32,8,256]{2,1,0:T(8,128)S(1)}, u32[]{:S(2)}) copy-start(f32[32,8,256]{2,1,0:T(8,128)S(1)} %get-tuple-element.42) | copy-start | bytes 786436
  23.7 2.9 %copy-start.25 = (f32[32,8]{1,0:T(8,128)}, f32[32,8]{1,0:T(8,128)S(1)}, u32[]{:S(2)}) copy-start(f32[32,8]{1,0:T(8,128)S(1)} %multiply_reduce_fusion.1) | copy-start | bytes 3076
  23.8 3.9 %copy-start.64 = (f32[16]{0:T(128)}, f32[16]{0:T(128)S(1)}, u32[]{:S(2)}) copy-start(f32[16]{0:T(128)S(1)} %convert_bitcast_fusion.2) | copy-start | bytes 196
  25.6 3.2 %copy-start.18 = (bf16[32,8,32]{2,1,0:T(8,128)(2,1)}, bf16[32,8,32]{2,1,0:T(8,128)(2,1)S(1)}, u32[]{:S(2)}) copy-start(bf16[32,8,32]{2,1,0:T(8,128)(2,1)S(1)} %get-tuple-element.7) | copy-start | bytes 49156
  28.9 180.8 %all-reduce.15.cloned.1.call-start = ((), (), s32[]{:S(2)}) async-start(), calls=%async_computation.2 | async-start | bytes 3801088 | tf_op jit(solution)/shard_map/psum | solution.py:145
  45.6 6.0 %copy-start.3 = (f32[32,8,256]{2,1,0:T(8,128)S(1)}, f32[32,8,256]{2,1,0:T(8,128)}, u32[]{:S(2)}) copy-start(f32[32,8,256]{2,1,0:T(8,128)} %copy-done.2) | copy-start | bytes 786436
  45.6 6.0 %copy-start.30 = (f32[32,8]{1,0:T(8,128)S(1)}, f32[32,8]{1,0:T(8,128)}, u32[]{:S(2)}) copy-start(f32[32,8]{1,0:T(8,128)} %copy-done.29) | copy-start | bytes 3076
  45.6 6.0 %copy-start.47 = (f32[32,8]{1,0:T(8,128)S(1)}, f32[32,8]{1,0:T(8,128)}, u32[]{:S(2)}) copy-start(f32[32,8]{1,0:T(8,128)} %copy-done.46) | copy-start | bytes 3076
  45.6 6.0 %copy-start.51 = (f32[32,8]{1,0:T(8,128)S(1)}, f32[32,8]{1,0:T(8,128)}, u32[]{:S(2)}) copy-start(f32[32,8]{1,0:T(8,128)} %copy-done.50) | copy-start | bytes 3076
  45.6 6.0 %copy-start.59 = (f32[1,256]{1,0:T(1,128)S(1)}, f32[1,256]{1,0:T(1,128)}, u32[]{:S(2)}) copy-start(f32[1,256]{1,0:T(1,128)} %get-tuple-element.28) | copy-start | bytes 3076
  45.6 6.0 %copy-start.76 = (bf16[256,64]{0,1:T(8,128)(2,1)S(1)}, bf16[256,64]{0,1:T(8,128)(2,1)}, u32[]{:S(2)}) copy-start(bf16[256,64]{0,1:T(8,128)(2,1)} %param.16) | copy-start | bytes 98308
  48.5 4.0 %copy-start.26 = (f32[32,8]{1,0:T(8,128)S(1)}, f32[32,8]{1,0:T(8,128)}, u32[]{:S(2)}) copy-start(f32[32,8]{1,0:T(8,128)} %copy-done.25) | copy-start | bytes 3076
  48.5 4.0 %copy-start.48 = (f32[32,8]{1,0:T(8,128)S(1)}, f32[32,8]{1,0:T(8,128)}, u32[]{:S(2)}) copy-start(f32[32,8]{1,0:T(8,128)} %copy-done.46) | copy-start | bytes 3076
  48.5 4.0 %copy-start.60 = (f32[1,256]{1,0:T(1,128)S(1)}, f32[1,256]{1,0:T(1,128)}, u32[]{:S(2)}) copy-start(f32[1,256]{1,0:T(1,128)} %get-tuple-element.28) | copy-start | bytes 3076
  50.0 2.9 %copy-start.11 = (bf16[1,32,8,256]{3,2,1,0:T(8,128)(2,1)S(1)}, bf16[1,32,8,256]{3,2,1,0:T(8,128)(2,1)}, u32[]{:S(2)}) copy-start(bf16[1,32,8,256]{3,2,1,0:T(8,128)(2,1)} %param.10) | copy-start | bytes 393220
  50.0 2.9 %copy-start.14 = (f32[256,256]{1,0:T(8,128)S(1)}, f32[256,256]{1,0:T(8,128)}, u32[]{:S(2)}) copy-start(f32[256,256]{1,0:T(8,128)} %get-tuple-element.40) | copy-start | bytes 786436
  52.9 2.7 %copy-start.24 = (f32[8,8,32]{2,1,0:T(8,128)S(1)}, f32[8,8,32]{2,1,0:T(8,128)}, u32[]{:S(2)}) copy-start(f32[8,8,32]{2,1,0:T(8,128)} %copy-done.23) | copy-start | bytes 24580
  52.9 2.7 %copy-start.34 = (f32[8,8,32]{2,1,0:T(8,128)S(1)}, f32[8,8,32]{2,1,0:T(8,128)}, u32[]{:S(2)}) copy-start(f32[8,8,32]{2,1,0:T(8,128)} %copy-done.33) | copy-start | bytes 24580
  60.9 3.5 %copy-start.17 = (bf16[5,256,256]{2,1,0:T(8,128)(2,1)S(1)}, bf16[5,256,256]{2,1,0:T(8,128)(2,1)}, u32[]{:S(2)}) copy-start(bf16[5,256,256]{2,1,0:T(8,128)(2,1)} %param.14) | copy-start | bytes 1966084
  64.4 3.4 %copy-start.20 = (bf16[32,8,8,32]{3,0,2,1:T(8,128)(2,1)S(1)}, bf16[32,8,8,32]{3,0,2,1:T(8,128)(2,1)}, u32[]{:S(2)}) copy-start(bf16[32,8,8,32]{3,0,2,1:T(8,128)(2,1)} %fusion.3) | copy-start | bytes 393220
  68.0 2.2 %copy-start.31 = (f32[32,8]{1,0:T(8,128)S(1)}, f32[32,8]{1,0:T(8,128)}, u32[]{:S(2)}) copy-start(f32[32,8]{1,0:T(8,128)} %copy-done.29) | copy-start | bytes 3076
  68.0 2.2 %copy-start.42 = (bf16[32,8,32]{2,1,0:T(8,128)(2,1)S(1)}, bf16[32,8,32]{2,1,0:T(8,128)(2,1)}, u32[]{:S(2)}) copy-start(bf16[32,8,32]{2,1,0:T(8,128)(2,1)} %copy-done.41) | copy-start | bytes 49156
  68.0 2.2 %copy-start.44 = (bf16[32,8,32]{2,1,0:T(8,128)(2,1)S(1)}, bf16[32,8,32]{2,1,0:T(8,128)(2,1)}, u32[]{:S(2)}) copy-start(bf16[32,8,32]{2,1,0:T(8,128)(2,1)} %copy-done.43) | copy-start | bytes 49156
  68.0 2.2 %copy-start.49 = (f32[32,8]{1,0:T(8,128)S(1)}, f32[32,8]{1,0:T(8,128)}, u32[]{:S(2)}) copy-start(f32[32,8]{1,0:T(8,128)} %copy-done.46) | copy-start | bytes 3076
  68.1 2.2 %copy-start.52 = (f32[32,8]{1,0:T(8,128)S(1)}, f32[32,8]{1,0:T(8,128)}, u32[]{:S(2)}) copy-start(f32[32,8]{1,0:T(8,128)} %copy-done.50) | copy-start | bytes 3076
  68.1 2.2 %copy-start.61 = (f32[1,256]{1,0:T(1,128)S(1)}, f32[1,256]{1,0:T(1,128)}, u32[]{:S(2)}) copy-start(f32[1,256]{1,0:T(1,128)} %get-tuple-element.28) | copy-start | bytes 3076
  68.1 2.2 %copy-start.69 = (f32[1,256]{1,0:T(1,128)S(1)}, f32[1,256]{1,0:T(1,128)}, u32[]{:S(2)}) copy-start(f32[1,256]{1,0:T(1,128)} %get-tuple-element.32) | copy-start | bytes 3076
  68.4 2.8 %copy-start.22 = (bf16[256,256]{1,0:T(8,128)(2,1)S(1)}, bf16[256,256]{1,0:T(8,128)(2,1)}, u32[]{:S(2)}) copy-start(bf16[256,256]{1,0:T(8,128)(2,1)} %copy-done.21) | copy-start | bytes 393220
  68.7 2.9 %copy-start.56 = (f32[1,256]{1,0:T(1,128)S(1)}, f32[1,256]{1,0:T(1,128)}, u32[]{:S(2)}) copy-start(f32[1,256]{1,0:T(1,128)} %copy-done.53) | copy-start | bytes 3076
  68.7 2.9 %copy-start.67 = (f32[1,256]{1,0:T(1,128)S(1)}, f32[1,256]{1,0:T(1,128)}, u32[]{:S(2)}) copy-start(f32[1,256]{1,0:T(1,128)} %copy-done.65) | copy-start | bytes 3076
  209.7 2.6 %copy-start.45 = (f32[256,64]{0,1:T(8,128)S(1)}, f32[256,64]{0,1:T(8,128)}, u32[]{:S(2)}) copy-start(f32[256,64]{0,1:T(8,128)} %get-tuple-element.54) | copy-start | bytes 196612
  209.7 3.2 %copy-start.19 = (f32[1024,128]{1,0:T(8,128)S(1)}, f32[1024,128]{1,0:T(8,128)}, u32[]{:S(2)}) copy-start(f32[1024,128]{1,0:T(8,128)} %get-tuple-element.55) | copy-start | bytes 1572868
  (31 other events, 38.8 us)
Sparse Core Ops, SparseCore 0:
  29.0 12.4 reduce-scatter.3
  74.4 135.1 all-reduce.14
where the time goes:
time: 221 us
  waiting for transfers between devices  92.4 us (42%)
  blocking collectives  47.8 us (22%)
  matrix products  28.2 us (13%)
  local copies, waits for them, and re-layouts  24.5 us (11%)
  between operations  15.2 us (7%)
  other arithmetic  12.4 us (6%)
    psum x1, waiting for transfers between devices, per_device(): lax.psum((focus_derivative, affine_derivative, factor_derivative, pair_we...  92.3 us
    psum x1, blocking collectives, per_device(): lax.psum((focus_derivative, affine_derivative, factor_derivative, pair_we...  41.5 us
    unnamed x160, local copies, waits for them, and re-layouts  9.1 us
    all_gather x1, blocking collectives, per_device(): right_all = lax.all_gather(right_own, 'axial', axis=1, tiled=True)  6.33 us
  transfers between devices with their start and end apart: 2, of which 1 were waited for; matrix products, arithmetic and copies ran while one was open for 7% of the time, Pallas kernels for 0%

commit v1 on v0

--- a/solution.py
+++ b/solution.py
@@ -142,9 +142,14 @@
     focus_derivative = attention_piece.astype(jnp.float32)
     affine_derivative = vector_piece
     factor_derivative = projection_piece.astype(jnp.float32)
-    focus_derivative, affine_derivative, factor_derivative, pair_weight_gradient = lax.psum(
-        (focus_derivative, affine_derivative, factor_derivative, pair_weight_gradient),
-        ("dp", "axial"),
+
+    def do_vector(load):
+        for dd in ("axial", "dp"):
+            load = lax.psum(load, axis_name=dd)
+        return load
+
+    focus_derivative, affine_derivative, factor_derivative, pair_weight_gradient = do_vector(
+        (focus_derivative, affine_derivative, factor_derivative, pair_weight_gradient)
     )
     return (
         alignment_piece[None],

time: 221 us -> 249 us (1.13)
  waiting for transfers between devices: 92.4 us -> 121 us
    psum x1 -> x2, waiting for transfers between devices: 92.3 us -> 120 us  [do_vector(): load = lax.psum(load, axis_name=dd)]
    psum x1 -> x2, blocking collectives: 41.5 us -> 38.9 us  [do_vector(): load = lax.psum(load, axis_name=dd)]
    unnamed x160 -> x146, local copies, waits for them, and re-layouts: 9.1 us -> 6.9 us
  transfers between devices with their start and end apart: 2 -> 3, of which waited for: 1 -> 2; matrix products, arithmetic and copies ran while one was open for 7% -> 6% of each run, Pallas kernels for 0% -> 0%
where the time goes in v1:
time: 249 us; the launch traced here: 248 us
  waiting for transfers between devices  121 us (49%)
  blocking collectives  46.9 us (19%)
  matrix products  29.5 us (12%)
  local copies, waits for them, and re-layouts  23.1 us (9%)
  between operations  15 us (6%)
  other arithmetic  13.2 us (5%)
    psum x2, waiting for transfers between devices, do_vector(): load = lax.psum(load, axis_name=dd)  120 us
    psum x2, blocking collectives, do_vector(): load = lax.psum(load, axis_name=dd)  38.9 us
    all_gather x1, blocking collectives, per_device(): right_all = lax.all_gather(right_own, 'axial', axis=1, tiled=True)  8.05 us
    unnamed x146, local copies, waits for them, and re-layouts  6.9 us
  transfers between devices with their start and end apart: 3, of which 2 were waited for; matrix products, arithmetic and copies ran while one was open for 6% of the time, Pallas kernels for 0%

profile of v1, /device:TPU:0, one launch (start us, length us, event | category | flops | bytes accessed | tf_op | source)
XLA Modules:
  0.0 248.3 jit_solution(14809274938996863928)
XLA Ops:
  7.2 1.1 convert_reduce_fusion
  8.3 1.1 fusion.48
  9.5 0.9 fusion.131
  10.4 1.2 fusion.11
  11.6 1.2 convolution_convert_fusion.18
  12.9 1.2 convolution_convert_fusion.19
  14.6 0.7 add_multiply_fusion
  15.6 0.8 fusion.133
  16.7 1.5 convolution_bitcast_fusion
  18.3 2.1 copy.86
  20.8 2.0 multiply_convert_fusion
  22.8 1.2 fusion.134
  25.4 0.7 fusion.130
  27.4 0.8 reshape.446
  28.5 0.8 reshape.467
  29.4 0.6 copy.88
  30.0 1.4 multiply_divide_fusion
  31.4 1.9 multiply_maximum_fusion
  33.3 8.0 %all_gather.3 = bf16[32,16,32]{2,1,0:T(8,128)(2,1)} all-gather(bf16[32,8,32]{2,1,0:T(8,128)(2,1)} %get-tuple-element.8), channel_id=1, replica_groups=mesh['dp'=16,'axial'=2] {'axial'}, dimensions={1}, use_global_device_ids=true | all-gather | bytes 49152 | tf_op jit(solution)/shard_map/all_gather | solution.py:121
  41.4 2.3 fusion
  43.7 1.6 copy.105
  45.3 1.8 convert_element_type.291
  47.1 0.9 broadcast_divide_fusion
  48.0 2.0 fusion.6
  50.1 1.4 convolution_bitcast_fusion.2
  51.5 0.7 div.102
  52.3 0.8 reshape.468
  53.2 1.7 fusion.69
  54.9 1.0 fusion.128
  56.0 1.8 fusion.135
  58.1 0.6 copy.94
  58.8 2.0 fusion.4
  60.8 0.6 fusion.31
  61.9 1.5 fusion.5
  63.4 1.5 fusion.3
  64.9 1.3 fusion.126
  66.2 2.0 copy.96
  68.7 1.2 copy.99
  71.5 1.3 fusion.51
  73.0 1.0 fusion.27
  75.8 1.2 add_convert_fusion
  77.1 59.4 %all-reduce.19.cloned.1.call-done = (f32[5,256,256]{2,1,0:T(8,128)}, f32[256,64]{0,1:T(8,128)}, f32[1024,128]{1,0:T(8,128)}) async-done(((f32[5,256,256]{2,1,0:T(8,128)}, f32[256,64]{0,1:T(8,128)}, f32[1024,128]{1,0:T(8,128)}), (f32[5,256,256]{2,1,0:T(8,128)}, f32[256,64]{0,1:T(8,128)}, f32[1024,128]{1,0:T(8,128)})) %all-reduce.19.cloned.1.call-update) | async-done | bytes 1900560 | tf_op jit(solution)/shard_map/psum | solution.py:148
  136.9 5.0 %psum.58 = f32[5,256]{1,0:T(8,128)S(1)} all-reduce(f32[5,256]{1,0:T(8,128)S(1)} %pad_add_fusion.3), channel_id=1, replica_groups=mesh['dp'=16,'axial'=2] {'axial'}, use_global_device_ids=true, to_apply=%region_20.0 | all-reduce | flops 1280 | bytes 10240 | tf_op jit(solution)/shard_map/psum | solution.py:148
  141.9 33.9 %psum.59 = f32[5,256]{1,0:T(8,128)} all-reduce(f32[5,256]{1,0:T(8,128)S(1)} %psum.58), channel_id=1, replica_groups=mesh['dp'=16,'axial'=2] {'dp'}, use_global_device_ids=true, to_apply=%region_21.0 | all-reduce | flops 1280 | bytes 10240 | tf_op jit(solution)/shard_map/psum | solution.py:148
  175.8 0.9 fusion.73
  176.7 61.1 %all-reduce.17.cloned.1.call-done = (f32[5,256,256]{2,1,0:T(8,128)}, f32[256,64]{0,1:T(8,128)}, f32[1024,128]{1,0:T(8,128)}) async-done(((f32[5,256,256]{2,1,0:T(8,128)}, f32[256,64]{0,1:T(8,128)}, f32[1024,128]{1,0:T(8,128)}), (f32[5,256,256]{2,1,0:T(8,128)}, f32[256,64]{0,1:T(8,128)}, f32[1024,128]{1,0:T(8,128)})) %all-reduce.17.cloned.1.call-update) | async-done | bytes 1900560 | tf_op jit(solution)/shard_map/psum | solution.py:148
  237.8 2.6 %copy.157 = f32[5,256,256]{2,1,0:T(8,128)} copy(f32[5,256,256]{2,1,0:T(8,128)} %get-tuple-element.55) | data formatting | bytes 2621440
  241.0 0.8 copy.159
  (198 shorter events, 10.1 us)
Async XLA Ops:
  7.2 20.0 %copy-start = (bf16[1024,128]{1,0:T(8,128)(2,1)S(1)}, bf16[1024,128]{1,0:T(8,128)(2,1)}, u32[]{:S(2)}) copy-start(bf16[1024,128]{1,0:T(8,128)(2,1)} %param.17) | copy-start | bytes 786436
  7.2 5.7 %copy-start.1 = (bf16[1,32,8,256]{3,2,1,0:T(8,128)(2,1)S(1)}, bf16[1,32,8,256]{3,2,1,0:T(8,128)(2,1)}, u32[]{:S(2)}) copy-start(bf16[1,32,8,256]{3,2,1,0:T(8,128)(2,1)} %param.9) | copy-start | bytes 393220
  7.2 45.1 %reduce-scatter.4.cloned.1.call-start = ((), (), s32[]{:S(2)}) async-start(), calls=%async_computation.1 | async-start | bytes 49152
  8.3 43.2 %copy-start.27 = (f32[32,8]{1,0:T(8,128)}, f32[32,8]{1,0:T(8,128)S(1)}, u32[]{:S(2)}) copy-start(f32[32,8]{1,0:T(8,128)S(1)} %broadcast_multiply_fusion.1) | copy-start | bytes 3076
  9.4 4.6 %copy-start.31 = (f32[32,8]{1,0:T(8,128)}, f32[32,8]{1,0:T(8,128)S(1)}, u32[]{:S(2)}) copy-start(f32[32,8]{1,0:T(8,128)S(1)} %fusion.48) | copy-start | bytes 3076
  9.4 11.3 %copy-start.41 = (f32[32,8]{1,0:T(8,128)}, f32[32,8]{1,0:T(8,128)S(1)}, u32[]{:S(2)}) copy-start(f32[32,8]{1,0:T(8,128)S(1)} %fusion.115) | copy-start | bytes 3076
  10.3 10.4 %copy-start.53 = (f32[1,256]{1,0:T(1,128)}, f32[1,256]{1,0:T(1,128)S(1)}, u32[]{:S(2)}) copy-start(f32[1,256]{1,0:T(1,128)S(1)} %get-tuple-element.34) | copy-start | bytes 3076
  10.3 10.4 %copy-start.62 = (f32[1,256]{1,0:T(1,128)}, f32[1,256]{1,0:T(1,128)S(1)}, u32[]{:S(2)}) copy-start(f32[1,256]{1,0:T(1,128)S(1)} %get-tuple-element.33) | copy-start | bytes 3076
  10.4 14.2 %copy-start.57 = (f32[1,256]{1,0:T(1,128)}, f32[1,256]{1,0:T(1,128)S(1)}, u32[]{:S(2)}) copy-start(f32[1,256]{1,0:T(1,128)S(1)} %get-tuple-element.31) | copy-start | bytes 3076
  10.4 14.2 %copy-start.64 = (f32[1,256]{1,0:T(1,128)}, f32[1,256]{1,0:T(1,128)S(1)}, u32[]{:S(2)}) copy-start(f32[1,256]{1,0:T(1,128)S(1)} %get-tuple-element.35) | copy-start | bytes 3076
  11.6 2.9 %copy-start.67 = (s32[1,32]{1,0:T(1,128)S(1)}, s32[1,32]{1,0:T(1,128)}, u32[]{:S(2)}) copy-start(s32[1,32]{1,0:T(1,128)} %param.12) | copy-start | bytes 388
  14.3 2.1 copy-start.4
  20.7 3.5 %copy-start.12 = (f32[256,256]{1,0:T(8,128)}, f32[256,256]{1,0:T(8,128)S(1)}, u32[]{:S(2)}) copy-start(f32[256,256]{1,0:T(8,128)S(1)} %reshape.445) | copy-start | bytes 786436
  20.8 3.5 %copy-start.68 = (s32[1,16]{1,0:T(1,128)S(1)}, s32[1,16]{1,0:T(1,128)}, u32[]{:S(2)}) copy-start(s32[1,16]{1,0:T(1,128)} %param.13) | copy-start | bytes 196
  20.8 4.3 %copy-start.69 = (bf16[256,64]{0,1:T(8,128)(2,1)S(1)}, bf16[256,64]{0,1:T(8,128)(2,1)}, u32[]{:S(2)}) copy-start(bf16[256,64]{0,1:T(8,128)(2,1)} %param.16) | copy-start | bytes 98308
  22.8 4.3 %copy-start.23 = (bf16[256,256]{1,0:T(8,128)(2,1)}, bf16[256,256]{1,0:T(8,128)(2,1)S(1)}, u32[]{:S(2)}) copy-start(bf16[256,256]{1,0:T(8,128)(2,1)S(1)} %get-tuple-element.42) | copy-start | bytes 393220
  22.8 4.2 %copy-start.39 = (bf16[1,8,16,128]{3,2,1,0:T(8,128)(2,1)S(1)}, bf16[1,8,16,128]{3,2,1,0:T(8,128)(2,1)}, u32[]{:S(2)}) copy-start(bf16[1,8,16,128]{3,2,1,0:T(8,128)(2,1)} %param.11) | copy-start | bytes 98308
  24.0 3.1 %copy-start.2 = (f32[32,8,256]{2,1,0:T(8,128)}, f32[32,8,256]{2,1,0:T(8,128)S(1)}, u32[]{:S(2)}) copy-start(f32[32,8,256]{2,1,0:T(8,128)S(1)} %get-tuple-element.45) | copy-start | bytes 786436
  24.2 2.9 %copy-start.29 = (f32[32,8]{1,0:T(8,128)}, f32[32,8]{1,0:T(8,128)S(1)}, u32[]{:S(2)}) copy-start(f32[32,8]{1,0:T(8,128)S(1)} %multiply_reduce_fusion.1) | copy-start | bytes 3076
  24.2 2.1 copy-start.48
  26.1 2.4 copy-start.20
  29.3 107.1 %all-reduce.19.cloned.1.call-start = ((), (), s32[]{:S(2)}) async-start(), calls=%async_computation.3 | async-start | bytes 3801088 | tf_op jit(solution)/shard_map/psum | solution.py:148
  47.1 6.0 %copy-start.3 = (f32[32,8,256]{2,1,0:T(8,128)S(1)}, f32[32,8,256]{2,1,0:T(8,128)}, u32[]{:S(2)}) copy-start(f32[32,8,256]{2,1,0:T(8,128)} %copy-done.2) | copy-start | bytes 786436
  47.1 6.1 %copy-start.34 = (f32[32,8]{1,0:T(8,128)S(1)}, f32[32,8]{1,0:T(8,128)}, u32[]{:S(2)}) copy-start(f32[32,8]{1,0:T(8,128)} %copy-done.33) | copy-start | bytes 3076
  47.1 6.1 %copy-start.49 = (f32[32,8]{1,0:T(8,128)S(1)}, f32[32,8]{1,0:T(8,128)}, u32[]{:S(2)}) copy-start(f32[32,8]{1,0:T(8,128)} %copy-done.48) | copy-start | bytes 3076
  50.1 4.8 %copy-start.30 = (f32[32,8]{1,0:T(8,128)S(1)}, f32[32,8]{1,0:T(8,128)}, u32[]{:S(2)}) copy-start(f32[32,8]{1,0:T(8,128)} %copy-done.29) | copy-start | bytes 3076
  51.5 4.5 %copy-start.10 = (bf16[1,32,8,256]{3,2,1,0:T(8,128)(2,1)S(1)}, bf16[1,32,8,256]{3,2,1,0:T(8,128)(2,1)}, u32[]{:S(2)}) copy-start(bf16[1,32,8,256]{3,2,1,0:T(8,128)(2,1)} %param.10) | copy-start | bytes 393220
  51.5 4.5 %copy-start.16 = (f32[256,256]{1,0:T(8,128)S(1)}, f32[256,256]{1,0:T(8,128)}, u32[]{:S(2)}) copy-start(f32[256,256]{1,0:T(8,128)} %get-tuple-element.43) | copy-start | bytes 786436
  52.2 2.7 %copy-start.43 = (bf16[32,8,32]{2,1,0:T(8,128)(2,1)}, bf16[32,8,32]{2,1,0:T(8,128)(2,1)S(1)}, u32[]{:S(2)}) copy-start(bf16[32,8,32]{2,1,0:T(8,128)(2,1)S(1)} %copy.144) | copy-start | bytes 49156
  54.9 3.0 %copy-start.14 = (f32[256,256]{1,0:T(8,128)}, f32[256,256]{1,0:T(8,128)S(1)}, u32[]{:S(2)}) copy-start(f32[256,256]{1,0:T(8,128)S(1)} %get-tuple-element.46) | copy-start | bytes 786436
  66.1 2.3 copy-start.19
  70.8 2.1 copy-start.35
  70.8 2.1 copy-start.44
  70.8 2.1 copy-start.46
  70.8 2.1 copy-start.50
  70.9 2.1 copy-start.52
  70.9 2.1 copy-start.58
  70.9 2.1 copy-start.65
  71.2 2.7 %copy-start.11 = (bf16[1,32,8,256]{3,2,1,0:T(8,128)(2,1)S(1)}, bf16[1,32,8,256]{3,2,1,0:T(8,128)(2,1)}, u32[]{:S(2)}) copy-start(bf16[1,32,8,256]{3,2,1,0:T(8,128)(2,1)} %param.10) | copy-start | bytes 393220
  71.3 2.7 %copy-start.24 = (bf16[256,256]{1,0:T(8,128)(2,1)S(1)}, bf16[256,256]{1,0:T(8,128)(2,1)}, u32[]{:S(2)}) copy-start(bf16[256,256]{1,0:T(8,128)(2,1)} %copy-done.23) | copy-start | bytes 393220
  71.5 2.7 %copy-start.55 = (f32[1,256]{1,0:T(1,128)S(1)}, f32[1,256]{1,0:T(1,128)}, u32[]{:S(2)}) copy-start(f32[1,256]{1,0:T(1,128)} %copy-done.53) | copy-start | bytes 3076
  71.5 2.7 %copy-start.63 = (f32[1,256]{1,0:T(1,128)S(1)}, f32[1,256]{1,0:T(1,128)}, u32[]{:S(2)}) copy-start(f32[1,256]{1,0:T(1,128)} %copy-done.62) | copy-start | bytes 3076
  77.0 59.5 %copy-start.15 = (f32[256,256]{1,0:T(8,128)S(1)}, f32[256,256]{1,0:T(8,128)}, u32[]{:S(2)}) copy-start(f32[256,256]{1,0:T(8,128)} %copy-done.14) | copy-start | bytes 786436
  77.0 59.9 %copy-start.60 = (f32[256]{0:T(256)S(1)}, f32[256]{0:T(256)}, u32[]{:S(2)}) copy-start(f32[256]{0:T(256)} %get-tuple-element.21) | copy-start | bytes 3076
  77.0 59.9 %copy-start.66 = (f32[256]{0:T(256)S(1)}, f32[256]{0:T(256)}, u32[]{:S(2)}) copy-start(f32[256]{0:T(256)} %get-tuple-element.9) | copy-start | bytes 3076
  77.0 160.8 %all-reduce.17.cloned.1.call-start = ((), (), s32[]{:S(2)}) async-start(), calls=%async_computation.2 | async-start | bytes 3801088 | tf_op jit(solution)/shard_map/psum | solution.py:148
  237.8 2.6 %copy-start.47 = (f32[256,64]{0,1:T(8,128)S(1)}, f32[256,64]{0,1:T(8,128)}, u32[]{:S(2)}) copy-start(f32[256,64]{0,1:T(8,128)} %get-tuple-element.57) | copy-start | bytes 196612
  237.8 3.2 %copy-start.21 = (f32[1024,128]{1,0:T(8,128)S(1)}, f32[1024,128]{1,0:T(8,128)}, u32[]{:S(2)}) copy-start(f32[1024,128]{1,0:T(8,128)} %get-tuple-element.58) | copy-start | bytes 1572868
  (25 other events, 38.2 us)
Sparse Core Ops, SparseCore 0:
  29.4 12.4 reduce-scatter.3
  77.1 59.2 all-reduce.18
  140.7 97.0 all-reduce.16
